TPU v7x, 256 devices: a whole 4x4x8 slice. The times are simulated.
256 devices in a mesh: tok: 16 (over y_lo, x, core), mdl: 16 (over y_hi, z).
Axes of the slice: x: 4, y: 4 (y_hi: 2, y_lo: 2; y = y_hi * 2 + y_lo), z: 8, core: 2. Of those that a mesh axis runs over, the one named last changes fastest.
Arguments:
- hidden: bfloat16 [8192, 2048], P('tok'), may hold values from -40 to 40
- segment_ids: int32 [8192], replicated, may hold values from 0 to 3, never falling along the last dimension, each value on 1 to 4096 neighbouring positions
- routes: int32 [8192, 2], P('tok'), may hold values from 0 to 7, all different within a row; in each aligned block of 512 rows (0 to 511, 512 to 1023, ...) at most 256 rows name the same one
- norm_gain: float32 [2048], replicated, may hold values from 0.5 to 1.5
- router_weight: float32 [2048, 8], replicated, may hold values from -0.125 to 0.125
- query_weight: bfloat16 [8, 2048, 2048], P(None, 'tok', 'mdl'), may hold values from -2 to 2
- kv_weight: bfloat16 [2, 2048, 2048], P(None, 'tok', 'mdl'), may hold values from -16 to 16
- out_weight: bfloat16 [8, 2048, 2048], P(None, 'mdl', 'tok'), may hold values from -0.5 to 0.5
- page_table: int32 [512], P('tok'), may hold values from 0 to 511, as said below
Outputs:
- output: bfloat16 [8192, 2048], P('tok', 'mdl')
- cache: bfloat16 [512, 16, 2, 2048], P('tok', None, None, 'mdl')
Inputs may be any that keep to these rules, and one draw needn't show every extreme that they name: `segment_ids`: Non-decreasing along the tokens; every prompt number 0 to 3 occurs, each prompt 1 to 4096 tokens long, one exactly 4096. `routes`: each token names 2 different experts; among the 512 tokens of an aligned block no expert is named more than 256 times, and some block reaches 256. `page_table`: A permutation of the 512 physical pages; of the 32 logical pages of each aligned block, exactly 2 lie in each aligned range of 32 physical pages.
All inputs are finite; a program needn't handle non-finite values.
Results may differ from a plain program's by a relative error of at most 0.019.
Values may be sent and summed in bfloat16 or wider, within the bound.
No kernel may reach another device: no remote copies, remote signals or barrier semaphores. Data moves between devices by JAX's collectives and lax.ppermute only.
A program may use at most 128 MiB of HBM per device.

v0:
```python
import math

import jax
import jax.numpy as jnp
from jax import lax
from jax.sharding import PartitionSpec as P

HDIM = 128
SEGS = 4


EPSILON = 1e-05
MASKED = -1e30


def rms_norm(hidden, norm_gain):
    values = hidden.astype(jnp.float32)
    factor = lax.rsqrt(jnp.mean(values * values, axis=-1, keepdims=True) + EPSILON)
    return (values * factor * norm_gain).astype(jnp.bfloat16)


def route_gates(normed, router_weight, routes):
    logits = jnp.dot(normed.astype(jnp.float32), router_weight, precision=lax.Precision.HIGHEST)
    expert_ids = jnp.arange(logits.shape[1], dtype=jnp.int32)
    picked = routes[:, :, None] == expert_ids[None, None, :]
    chosen = jnp.sum(jnp.where(picked, logits[:, None, :], jnp.float32(0.0)), axis=-1)
    return jax.nn.softmax(chosen, axis=-1)


def place_pages(key_values, page_table, shards, tok_row):
    pages_here = page_table.shape[0]
    per_peer = pages_here // shards
    page_rows = key_values.shape[0] // pages_here
    head_cols = key_values.shape[2]
    targets = page_table // pages_here
    onehot = (targets[:, None] == jnp.arange(shards, dtype=jnp.int32)[None, :]).astype(jnp.int32)
    ranks = jnp.sum((jnp.cumsum(onehot, axis=0) - 1) * onehot, axis=1)
    ordering = (
        jnp.zeros((pages_here,), jnp.int32)
        .at[targets * per_peer + ranks]
        .set(jnp.arange(pages_here, dtype=jnp.int32))
    )
    outgoing = key_values.reshape(pages_here, page_rows, 2, head_cols)[ordering].reshape(
        shards, per_peer, page_rows, 2, head_cols
    )
    labels = page_table[ordering].reshape(shards, per_peer)
    incoming, got_labels = (
        lax.all_to_all(outgoing, "tok", split_axis=0, concat_axis=0, tiled=True),
        lax.all_to_all(labels, "tok", split_axis=0, concat_axis=0, tiled=True),
    )
    places = got_labels.reshape(-1) - tok_row * pages_here
    arrived = incoming.reshape(pages_here, page_rows, 2, head_cols)
    return jnp.zeros((pages_here, page_rows, 2, head_cols), jnp.bfloat16).at[places].set(arrived)


def local(
    hidden,
    segment_ids,
    routes,
    norm_gain,
    router_weight,
    query_weight,
    kv_weight,
    out_weight,
    page_table,
):
    tok_dev, width = hidden.shape
    experts = query_weight.shape[0]
    head_cols = query_weight.shape[2]
    heads_here = head_cols // HDIM
    capacity = tok_dev // 2
    top_count = routes.shape[1]
    assigned = tok_dev * top_count
    shards = lax.axis_size("tok")
    tok_row = lax.axis_index("tok")
    normed = rms_norm(hidden, norm_gain)
    gates = route_gates(normed, router_weight, routes)
    flat_expert = routes.reshape(-1)
    expert_ids = jnp.arange(experts, dtype=jnp.int32)
    onehot = (flat_expert[:, None] == expert_ids[None, :]).astype(jnp.int32)
    ranks = jnp.sum((jnp.cumsum(onehot, axis=0) - 1) * onehot, axis=1)
    slots = flat_expert * capacity + ranks
    assign_ids = jnp.arange(assigned, dtype=jnp.int32)
    slot_assign = jnp.zeros((experts * capacity,), jnp.int32).at[slots].set(assign_ids)
    slot_token = slot_assign // top_count
    slot_filled = jnp.zeros((experts * capacity,), jnp.bfloat16).at[slots].set(jnp.bfloat16(1.0))
    slot_gate = jnp.zeros((experts * capacity,), jnp.float32).at[slots].set(gates.reshape(-1))
    grouped = (normed[slot_token] * slot_filled[:, None]).reshape(experts, capacity, width)
    query_part = lax.all_gather(query_weight, "tok", axis=1, tiled=True)
    key_part = lax.all_gather(kv_weight, "tok", axis=1, tiled=True)
    query_total = jnp.einsum(
        "ecd,edh->ech", grouped, query_part, preferred_element_type=jnp.float32
    )
    key_total = jnp.einsum("td,kdh->tkh", normed, key_part, preferred_element_type=jnp.float32)
    queries = query_total.astype(jnp.bfloat16).reshape(experts * capacity, head_cols)[slots]
    key_values = key_total.astype(jnp.bfloat16)
    cache = place_pages(key_values, page_table, shards, tok_row)
    by_head_q = queries.reshape(assigned, heads_here, HDIM).transpose(1, 0, 2)
    q_pos = tok_row * tok_dev + assign_ids // top_count
    q_seg = segment_ids[q_pos]
    prompt_ids = jnp.arange(SEGS, dtype=jnp.int32)
    seg_first = jnp.sum((segment_ids[:, None] < prompt_ids[None, :]).astype(jnp.int32), axis=0)
    q_lower = jnp.sum(
        jnp.where(q_seg[:, None] == prompt_ids[None, :], seg_first[None, :], 0), axis=1
    )
    start_state = (
        jnp.full((heads_here, assigned), MASKED, jnp.float32),
        jnp.zeros((heads_here, assigned), jnp.float32),
        jnp.zeros((heads_here, assigned, HDIM), jnp.float32),
    )
    state = start_state
    piece = lax.all_gather(key_values, "tok", axis=0, tiled=True)
    count = piece.shape[0]
    block = math.gcd(count, 512)
    key_blocks = piece[:, 0].reshape(count // block, block, heads_here, HDIM)
    value_blocks = piece[:, 1].reshape(count // block, block, heads_here, HDIM)
    firsts = block * jnp.arange(count // block, dtype=jnp.int32)

    def one_block(carry, inputs):
        peak, total, accum = carry
        key_block, value_block, first = inputs
        k_pos = first + jnp.arange(block, dtype=jnp.int32)
        allowed = (k_pos[None, :] >= q_lower[:, None]) & (k_pos[None, :] <= q_pos[:, None])
        scores = jnp.einsum(
            "hqd,khd->hqk", by_head_q, key_block, preferred_element_type=jnp.float32
        ) / math.sqrt(HDIM)
        scores = jnp.where(allowed[None], scores, jnp.float32(MASKED))
        new_peak = jnp.maximum(peak, jnp.max(scores, axis=-1))
        shrink = jnp.exp(peak - new_peak)
        expon = jnp.where(allowed[None], jnp.exp(scores - new_peak[..., None]), jnp.float32(0.0))
        total = total * shrink + jnp.sum(expon, axis=-1)
        accum = accum * shrink[..., None] + jnp.einsum(
            "hqk,khd->hqd",
            expon.astype(jnp.bfloat16),
            value_block,
            preferred_element_type=jnp.float32,
        )
        return ((new_peak, total, accum), None)

    state, _ = lax.scan(one_block, state, (key_blocks, value_blocks, firsts))
    attended = (
        (state[2] / state[1][..., None])
        .astype(jnp.bfloat16)
        .transpose(1, 0, 2)
        .reshape(assigned, head_cols)
    )
    grouped_out = (attended[slot_assign] * slot_filled[:, None]).reshape(
        experts, capacity, head_cols
    )
    piece = lax.all_gather(out_weight, "tok", axis=2, tiled=True)
    count = piece.shape[2]
    terms = jnp.einsum(
        "ech,ehn->ecn", grouped_out, piece, preferred_element_type=jnp.float32
    ).reshape(experts * capacity, count)
    partial_sums = (
        jnp.zeros((tok_dev, count), jnp.float32).at[slot_token].add(terms * slot_gate[:, None])
    )
    mine = lax.psum_scatter(
        partial_sums.astype(jnp.bfloat16), "mdl", scatter_dimension=1, tiled=True
    ).astype(jnp.float32)
    span = width // lax.axis_size("mdl")
    residual_part = lax.dynamic_slice_in_dim(hidden, lax.axis_index("mdl") * span, span, 1)
    output = (residual_part.astype(jnp.float32) + mine).astype(jnp.bfloat16)
    return (output, cache)


def solution(mesh):
    placed = (
        P("tok", None),
        P(),
        P("tok", None),
        P(),
        P(),
        P(None, "tok", "mdl"),
        P(None, "tok", "mdl"),
        P(None, "mdl", "tok"),
        P("tok"),
    )
    return jax.shard_map(
        local,
        mesh=mesh,
        in_specs=placed,
        out_specs=(P("tok", "mdl"), P("tok", None, None, "mdl")),
        check_vma=False,
    )
```

profile of v0, /device:TPU:9, one launch (start us, length us, event | category | flops | bytes accessed | tf_op | source)
XLA Modules:
  0.0 469.7 jit_solution(12940662665245141497)
XLA Ops:
  11.6 36.2 %all-gather.5.cloned.1.call-done = bf16[2,2048,128]{2,1,0:T(8,128)(2,1)} async-done(((bf16[2,128,128]{2,1,0:T(8,128)(2,1)}), bf16[2,2048,128]{2,1,0:T(8,128)(2,1)}) %all-gather.5.cloned.1.call-update) | async-done | bytes 1048592 | tf_op jit(solution)/shard_map/all_gather | solution.py:90
  47.8 2.6 fusion.45
  51.9 6.2 %gather_fusion = s32[1024]{0:T(1024)S(1)} fusion(s32[8192]{0:T(1024)S(1)} %copy-done.2, s32[1024]{0:T(1024)S(1)} %broadcast_clamp_fusion.2), kind=kCustom, calls=%fused_computation | custom fusion | bytes 12288 | tf_op jit(solution)/shard_map/gather | solution.py:100
  58.4 2.3 reduce-window.6
  61.2 7.6 %scatter_custom_fusion.1 = bf16[2048]{0:T(1024)(128)(2,1)S(1)} fusion(s32[1024]{0:T(1024)S(1)} %bitcast.131, bf16[1024]{0:T(1024)(128)(2,1)S(1)} %broadcast.244, bf16[]{:T(256)} %constant.112.clone.1), kind=kCustom, calls=%fused_computation.125 | custom fusion | bytes 4098 | tf_op jit(solution)/shard_map/scatter | solution.py:86
  68.9 4.3 scatter_custom_fusion
  75.4 11.0 %gather_fusion.1 = bf16[2048,2048]{1,0:T(8,128)(2,1)} fusion(bf16[512,2048]{1,0:T(8,128)(2,1)S(1)} %fusion.36, s32[2048]{0:T(1024)S(1)} %get-tuple-element.163), kind=kCustom, calls=%fused_computation.1 | custom fusion | bytes 16785408 | tf_op jit(solution)/shard_map/gather | solution.py:88
  86.5 4.5 scatter_custom_fusion.2
  91.0 7.0 %fusion.42 = bf16[8,256,128]{2,1,0:T(8,128)(2,1)S(1)} fusion(bf16[8,2048,128]{2,1,0:T(8,128)(2,1)} %all-gather.9.cloned.1.call-done, bf16[8,256,2048]{2,1,0:T(8,128)(2,1)} %bitcast.113, bf16[8,256]{1,0:T(8,128)(2,1)S(1)} %mul.112), kind=kOutput, calls=%fused_computation.68 | convolution fusion | flops 1078198272 | bytes 13111296 | tf_op jit(solution)/shard_map/ecd,edh->ech/dot_general | solution.py:91
  98.0 3.2 gather_fusion.2
  101.2 31.0 %all-gather.7.cloned.1.call-done = bf16[8192,2,128]{2,0,1:T(8,128)(2,1)} async-done(((bf16[512,2,128]{2,0,1:T(8,128)(2,1)}), bf16[8192,2,128]{2,0,1:T(8,128)(2,1)}) %all-gather.7.cloned.1.call-update) | async-done | bytes 4194320 | tf_op jit(solution)/shard_map/all_gather | solution.py:112
  132.2 3.8 fusion.71
  136.0 73.6 %while.15 = (s32[]{:T(128)}, f32[1,1024]{1,0:T(1,128)S(1)}, f32[1,1024]{1,0:T(1,128)S(1)}, f32[1,1024,128]{2,1,0:T(8,128)S(1)}, s32[16]{0:T(128)S(1)}, /*index=5...) while((s32[]{:T(128)}, f32[1,1024]{1,0:T(1,128)S(1)}, ...), condition=%wide.region_11.12_spmd.clone, body=%wide.region_8.11_spmd.clone.sunk | while | flops 280377856 | bytes 7966885 | solution.py:140
  209.9 6.2 %gather_fusion.3 = bf16[2048,128]{1,0:T(8,128)(2,1)S(1)} fusion(bf16[1024,128]{1,0:T(8,128)(2,1)S(1)} %fusion.51, s32[2048]{0:T(1024)S(1)} %get-tuple-element.169), kind=kCustom, calls=%fused_computation.3 | custom fusion | bytes 1056768 | tf_op jit(solution)/shard_map/gather | solution.py:147
  216.1 4.6 fusion.48
  220.7 7.1 %bitcast_multiply_fusion = f32[2048,2048]{1,0:T(8,128)} fusion(f32[8,256,2048]{2,1,0:T(8,128)S(1)} %fusion.48, f32[2048]{0:T(1024)S(1)} %scatter_custom_fusion.2), kind=kLoop, calls=%fused_computation.55 | loop fusion | flops 4194304 | bytes 33562624 | tf_op jit(solution)/shard_map/mul | solution.py:156
  227.8 29.5 %scatter_custom_fusion.3 = f32[512,2048]{1,0:T(8,128)} fusion(s32[2048]{0:T(1024)S(1)} %get-tuple-element.164, f32[2048,2048]{1,0:T(8,128)} %bitcast_multiply_fusion, f32[]{:T(128)} %constant.102.clone.1), kind=kCustom, calls=%fused_computation.66 | custom fusion | flops 4194304 | bytes 4194816 | tf_op jit(solution)/shard_map/scatter-add | solution.py:156
  257.3 2.5 convert_element_type.51
  259.8 2.5 copy.41
  265.4 4.7 all-to-all-start
  271.4 3.0 all-to-all-done
  274.4 5.1 %all-to-all-start.1 = ((bf16[16,2,16,2,128]{4,2,3,1,0:T(8,128)(2,1)}), bf16[16,2,16,2,128]{4,2,3,1,0:T(8,128)(2,1)S(1)}, u32[]{:S(2)}, u32[]{:S(2)}) async-start(bf16[16,2,16,2,128]{4,2,3,1,0:T(8,128)(2,1)} %bitcast.19), calls=%async_computation.1 | async-start | bytes 524288 | tf_op jit(solution)/shard_map/all_to_all | solution.py:48
  279.7 6.4 %all-to-all-done.1 = bf16[16,2,16,2,128]{4,2,3,1,0:T(8,128)(2,1)S(1)} async-done(((bf16[16,2,16,2,128]{4,2,3,1,0:T(8,128)(2,1)}), bf16[16,2,16,2,128]{4,2,3,1,0:T(8,128)(2,1)S(1)}, u32[]{:S(2)}, u32[]{:S(2)}) %all-to-all-start.1) | async-done | bytes 262176 | tf_op jit(solution)/shard_map/all_to_all | solution.py:48
  288.5 172.0 %reduce-scatter.4.cloned.1.call-done = bf16[128,512]{1,0:T(8,128)(2,1)} async-done(((bf16[2048,512]{1,0:T(8,128)(2,1)}), bf16[128,512]{1,0:T(8,128)(2,1)}) %reduce-scatter.4.cloned.1.call-update) | async-done | bytes 131088
  (228 shorter events, 91.2 us)
Async XLA Ops:
  7.2 66.0 %copy-start = (f32[2048,8]{0,1:T(8,128)S(1)}, f32[2048,8]{0,1:T(8,128)}, u32[]{:S(2)}) copy-start(f32[2048,8]{0,1:T(8,128)} %param.15) | copy-start | bytes 196612
  7.2 3.8 copy-start.7
  7.2 40.6 %all-gather.5.cloned.1.call-start = ((), (), s32[]{:S(2)}) async-start(), calls=%async_computation.3 | async-start | bytes 1114112 | tf_op jit(solution)/shard_map/all_gather | solution.py:90
  7.9 83.1 %all-gather.9.cloned.1.call-start = ((), (), s32[]{:S(2)}) async-start(), calls=%async_computation.5 | async-start | bytes 4456448 | tf_op jit(solution)/shard_map/all_gather | solution.py:89
  8.7 123.5 %all-gather.7.cloned.1.call-start = ((), (), s32[]{:S(2)}) async-start(), calls=%async_computation.4 | async-start | bytes 4456448 | tf_op jit(solution)/shard_map/all_gather | solution.py:112
  8.7 2.3 copy-start.4
  11.5 39.6 %copy-start.6 = (s32[512,2]{0,1:T(2,128)S(1)}, s32[512,2]{0,1:T(2,128)}, u32[]{:S(2)}) copy-start(s32[512,2]{0,1:T(2,128)} %param.13) | copy-start | bytes 12292
  11.5 40.1 %copy-start.2 = (s32[8192]{0:T(1024)S(1)}, s32[8192]{0:T(1024)}, u32[]{:S(2)}) copy-start(s32[8192]{0:T(1024)} %param.12) | copy-start | bytes 98308
  50.4 165.6 %all-gather.11.cloned.1.call-start = ((), (), s32[]{:S(2)}) async-start(), calls=%async_computation.6 | async-start | bytes 4456448 | tf_op jit(solution)/shard_map/all_gather | solution.py:150
  51.0 409.5 %reduce-scatter.4.cloned.1.call-start = ((), (), s32[]{:S(2)}) async-start(), calls=%async_computation.7 | async-start | bytes 2228224
  262.3 0.7 copy-start.3
  262.3 7.8 %copy-start.5 = (bf16[512,2,128]{2,0,1:T(8,128)(2,1)S(1)}, bf16[512,2,128]{2,0,1:T(8,128)(2,1)}, u32[]{:S(2)}) copy-start(bf16[512,2,128]{2,0,1:T(8,128)(2,1)} %fusion.45) | copy-start | bytes 786436
  262.9 200.2 %copy-start.1 = (f32[2048,8]{0,1:T(8,128)S(1)}, f32[2048,8]{0,1:T(8,128)}, u32[]{:S(2)}) copy-start(f32[2048,8]{0,1:T(8,128)} %param.15) | copy-start | bytes 196612
  265.4 9.0 %all-to-all-start = ((s32[16,1,2]{2,1,0:T(1,128)}), s32[16,1,2]{2,1,0:T(1,128)S(1)}, u32[]{:S(2)}, u32[]{:S(2)}) async-start(s32[16,1,2]{2,1,0:T(1,128)} %bitcast.16), calls=%async_computation | async-start | bytes 16384 | tf_op jit(solution)/shard_map/all_to_all | solution.py:49
  274.4 11.6 %all-to-all-start.1 = ((bf16[16,2,16,2,128]{4,2,3,1,0:T(8,128)(2,1)}), bf16[16,2,16,2,128]{4,2,3,1,0:T(8,128)(2,1)S(1)}, u32[]{:S(2)}, u32[]{:S(2)}) async-start(bf16[16,2,16,2,128]{4,2,3,1,0:T(8,128)(2,1)} %bitcast.19), calls=%async_computation.1 | async-start | bytes 524288 | tf_op jit(solution)/shard_map/all_to_all | solution.py:48
Sparse Core Ops, SparseCore 0:
  9.8 37.9 all-gather.4
  49.6 40.1 all-gather.8
  92.1 39.9 all-gather.6
  133.8 47.7 all-gather.10
  262.4 198.0 reduce-scatter.3
where the time goes:
time: 477 us; the launch traced here: 470 us
  waiting for transfers between devices  251 us (53%)
  other arithmetic  69.7 us (15%)
  local copies, waits for them, and re-layouts  67.9 us (14%)
  matrix products  56.2 us (12%)
  between operations  14.2 us (3%)
  starting transfers between devices  10 us (2%)
    unnamed x6, waiting for transfers between devices  174 us
    all_gather x1, waiting for transfers between devices, local(): key_part = lax.all_gather(kv_weight, 'tok', axis=1, tiled=True)  36.2 us
    all_gather x1, waiting for transfers between devices, local(): piece = lax.all_gather(key_values, 'tok', axis=0, tiled=True)  31 us
    scatter-add x1, other arithmetic, local(): jnp.zeros((tok_dev, count), jnp.float32).at[slot_token]  29.5 us
    dot_general x16, matrix products, one_block(): jnp.einsum('hqd,khd->hqk', by_head_q, key_block, preferred_element_type=j...  24.3 us
    dot_general x16, matrix products, one_block(): jnp.einsum('hqk,khd->hqd', expon.astype(jnp.bfloat16), value_block, prefe...  16 us
    reduce_sum x16, other arithmetic, one_block(): total = total * shrink + jnp.sum(expon, axis=-1)  12.1 us
    gather x1, local copies, waits for them, and re-layouts, local(): normed[slot_token] * slot_filled[:, None]  11 us
  transfers between devices with their start and end apart: 7, of which 5 were waited for; matrix products, arithmetic and copies ran while one was open for 31% of the time, Pallas kernels for 0%

commit v1 on v0

v1 whole, which is shorter than its diff:
```python
import math

import jax
import jax.numpy as jnp
from jax import lax
from jax.experimental import pallas as pl
from jax.experimental.pallas import tpu as pltpu
from jax.sharding import PartitionSpec as P

HDIM = 128
SEGS = 4
EPSILON = 1e-05
MASKED = -1e30
KEY_BLOCK = 512
QUERY_BLOCK = 256
WINDOW_PAIRS = 5
QUERY_SCALE = math.log2(math.e) / math.sqrt(HDIM)


def rms_norm(hidden, norm_gain):
    values = hidden.astype(jnp.float32)
    factor = lax.rsqrt(jnp.mean(values * values, axis=-1, keepdims=True) + EPSILON)
    return (values * factor * norm_gain).astype(jnp.bfloat16)


def route_weights(normed, router_weight, routes):
    logits = jnp.dot(normed.astype(jnp.float32), router_weight, precision=lax.Precision.HIGHEST)
    expert_ids = jnp.arange(logits.shape[1], dtype=jnp.int32)
    picked = routes[:, :, None] == expert_ids[None, None, :]
    chosen = jnp.sum(jnp.where(picked, logits[:, None, :], jnp.float32(0.0)), axis=-1)
    gates = jax.nn.softmax(chosen, axis=-1)
    return jnp.where(picked, gates[:, :, None], 0.0).reshape(routes.shape[0], -1)


def place_pages(key_values, page_table, shards, tok_row):
    pages_here = page_table.shape[0]
    per_peer = pages_here // shards
    rows = key_values.shape[0] // pages_here
    cols = key_values.shape[1]
    targets = page_table // pages_here
    onehot = (targets[:, None] == jnp.arange(shards, dtype=jnp.int32)[None, :]).astype(jnp.int32)
    ranks = jnp.sum((jnp.cumsum(onehot, axis=0) - 1) * onehot, axis=1)
    ordering = (
        jnp.zeros((pages_here,), jnp.int32)
        .at[targets * per_peer + ranks]
        .set(jnp.arange(pages_here, dtype=jnp.int32))
    )
    outgoing = key_values.reshape(pages_here, rows, cols)[ordering].reshape(
        shards, per_peer, rows, cols
    )
    labels = page_table[ordering].reshape(shards, per_peer)
    incoming = lax.all_to_all(outgoing, "tok", split_axis=0, concat_axis=0, tiled=True)
    got_labels = lax.all_to_all(labels, "tok", split_axis=0, concat_axis=0, tiled=True)
    places = got_labels.reshape(-1) - tok_row * pages_here
    order = jnp.zeros((pages_here,), jnp.int32).at[places].set(
        jnp.arange(pages_here, dtype=jnp.int32)
    )
    return incoming.reshape(pages_here, rows, 2, cols // 2)[order]


def query_body(normed_ref, weight_ref, routes_ref, out_ref):
    step = pl.program_id(0)
    chunks, pair, rows, cols = weight_ref.shape
    weights = [weight_ref[:, k].reshape(chunks * rows, cols) for k in range(pair)]
    total = jnp.dot(
        normed_ref[...], jnp.concatenate(weights, axis=1), preferred_element_type=jnp.float32
    )
    for s in range(out_ref.shape[0]):
        route = routes_ref[:, s : s + 1]
        value = out_ref[s]
        for k in range(pair):
            mine = (total[:, k * cols : (k + 1) * cols] * QUERY_SCALE).astype(jnp.bfloat16)
            value = jnp.where(route == step * pair + k, mine, value)
        out_ref[s] = value


def project_queries(normed, gathered, routes, experts):
    tokens, width = normed.shape
    shards, _, rows, cols = gathered.shape
    return pl.pallas_call(
        query_body,
        grid=(experts // 2,),
        in_specs=[
            pl.BlockSpec((tokens, width), lambda e: (0, 0)),
            pl.BlockSpec((shards, 2, rows, cols), lambda e: (0, e, 0, 0)),
            pl.BlockSpec(routes.shape, lambda e: (0, 0)),
        ],
        out_specs=pl.BlockSpec((routes.shape[1], tokens, cols), lambda e: (0, 0, 0)),
        out_shape=jax.ShapeDtypeStruct((routes.shape[1], tokens, cols), jnp.bfloat16),
    )(normed, gathered, routes)


def attend_body(bounds_ref, q_ref, lower_ref, place_ref, kv_ref, out_ref):
    step = pl.program_id(0)
    routes, tokens, dim = q_ref.shape
    rows = routes * tokens
    q = q_ref[...].reshape(rows, dim)
    lower = jnp.concatenate([lower_ref[...]] * routes, axis=0)
    place = jnp.concatenate([place_ref[...]] * routes, axis=0)

    def block(masked, at, carry):
        peak, total, accum = carry
        first = pl.multiple_of(at * KEY_BLOCK, KEY_BLOCK)
        keys = kv_ref[pl.ds(first, KEY_BLOCK), :dim]
        values = kv_ref[pl.ds(first, KEY_BLOCK), dim:]
        scores = lax.dot_general(
            q, keys, (((1,), (1,)), ((), ())), preferred_element_type=jnp.float32
        )
        if masked:
            key_place = first + lax.broadcasted_iota(jnp.int32, (1, KEY_BLOCK), 1)
            allowed = (key_place >= lower) & (key_place <= place)
            scores = jnp.where(allowed, scores, MASKED)
        new_peak = jnp.maximum(peak, jnp.max(scores, axis=1, keepdims=True))
        shrink = jnp.exp2(peak - new_peak)
        expon = jnp.exp2(scores - new_peak)
        total = total * shrink + jnp.sum(expon, axis=1, keepdims=True)
        accum = accum * shrink + jnp.dot(
            expon.astype(jnp.bfloat16), values, preferred_element_type=jnp.float32
        )
        return new_peak, total, accum

    state = (
        jnp.full((rows, 1), MASKED, jnp.float32),
        jnp.zeros((rows, 1), jnp.float32),
        jnp.zeros((rows, dim), jnp.float32),
    )
    start, full, edge, stop = (bounds_ref[4 * step + k] for k in range(4))
    state = lax.fori_loop(start, full, lambda at, c: block(True, at, c), state)
    state = lax.fori_loop(full, edge, lambda at, c: block(False, at, c), state)
    state = lax.fori_loop(edge, stop, lambda at, c: block(True, at, c), state)
    out_ref[...] = (state[2] / state[1]).astype(jnp.bfloat16).reshape(routes, tokens, dim)


def attend(queries, lower, place, window):
    routes, tokens, dim = queries.shape
    steps = tokens // QUERY_BLOCK
    first_lower = lower.reshape(steps, QUERY_BLOCK)[:, 0]
    last_lower = lower.reshape(steps, QUERY_BLOCK)[:, -1]
    first_place = place.reshape(steps, QUERY_BLOCK)[:, 0]
    last_place = place.reshape(steps, QUERY_BLOCK)[:, -1]
    start = first_lower // KEY_BLOCK
    stop = last_place // KEY_BLOCK + 1
    full = jnp.clip((last_lower + KEY_BLOCK - 1) // KEY_BLOCK, start, stop)
    edge = jnp.clip((first_place + 1) // KEY_BLOCK, full, stop)
    bounds = jnp.stack([start, full, edge, stop], axis=1).reshape(-1)
    return pl.pallas_call(
        attend_body,
        grid_spec=pltpu.PrefetchScalarGridSpec(
            num_scalar_prefetch=1,
            grid=(steps,),
            in_specs=[
                pl.BlockSpec((routes, QUERY_BLOCK, dim), lambda i, b: (0, i, 0)),
                pl.BlockSpec((QUERY_BLOCK, 1), lambda i, b: (i, 0)),
                pl.BlockSpec((QUERY_BLOCK, 1), lambda i, b: (i, 0)),
                pl.BlockSpec(window.shape, lambda i, b: (0, 0)),
            ],
            out_specs=pl.BlockSpec((routes, QUERY_BLOCK, dim), lambda i, b: (0, i, 0)),
        ),
        out_shape=jax.ShapeDtypeStruct((routes, tokens, dim), jnp.bfloat16),
    )(bounds, queries, lower[:, None], place[:, None], window)


def mix_body(side_ref, own_ref, peer_ref, gates_ref, own_weight_ref, peer_weight_ref, out_ref, mix_ref):
    del side_ref
    experts, rows, cols = own_weight_ref.shape[2:]
    routes = own_ref.shape[0]

    @pl.when(pl.program_id(0) == 0)
    def _():
        for h, ref in enumerate((own_ref, peer_ref)):
            attended = [ref[s].astype(jnp.float32) for s in range(routes)]
            for e in range(experts):
                value = sum(
                    attended[s] * gates_ref[:, s * experts + e : s * experts + e + 1]
                    for s in range(routes)
                )
                mix_ref[h, :, e * rows : (e + 1) * rows] = value.astype(jnp.bfloat16)

    total = jnp.zeros((out_ref.shape[1], 2 * cols), jnp.float32)
    for h, ref in enumerate((own_weight_ref, peer_weight_ref)):
        weight = jnp.concatenate(
            [ref[0, k].reshape(experts * rows, cols) for k in range(2)], axis=1
        )
        total = total + jnp.dot(mix_ref[h], weight, preferred_element_type=jnp.float32)
    for k in range(2):
        out_ref[k] = total[:, k * cols : (k + 1) * cols].astype(jnp.bfloat16)


def mix_heads(side, own, peer, gates, gathered, experts):
    routes, tokens, dim = own.shape
    _, chunks, _, rows, cols = gathered.shape
    block = (1, 2, experts, rows, cols)
    whole = lambda i, s: (0, 0, 0)
    return pl.pallas_call(
        mix_body,
        grid_spec=pltpu.PrefetchScalarGridSpec(
            num_scalar_prefetch=1,
            grid=(chunks // 2,),
            in_specs=[
                pl.BlockSpec((routes, tokens, dim), whole),
                pl.BlockSpec((routes, tokens, dim), whole),
                pl.BlockSpec(gates.shape, lambda i, s: (0, 0)),
                pl.BlockSpec(block, lambda i, s: (s[0], i, 1, 0, 0)),
                pl.BlockSpec(block, lambda i, s: (1 - s[0], i, 1, 0, 0)),
            ],
            out_specs=pl.BlockSpec((2, tokens, cols), lambda i, s: (i, 0, 0)),
            scratch_shapes=[pltpu.VMEM((2, tokens, experts * rows), jnp.bfloat16)],
        ),
        out_shape=jax.ShapeDtypeStruct((chunks, tokens, cols), jnp.bfloat16),
    )(side, own, peer, gates, gathered, gathered)


def local(
    hidden,
    segment_ids,
    routes,
    norm_gain,
    router_weight,
    query_weight,
    kv_weight,
    out_weight,
    page_table,
):
    tok_dev, width = hidden.shape
    experts, chunk, head_cols = query_weight.shape
    shards = lax.axis_size("tok")
    groups = lax.axis_size("mdl")
    half_tok, half_mdl = shards // 2, groups // 2
    tok_row = lax.axis_index("tok")
    mdl_row = lax.axis_index("mdl")
    core = tok_row % 2
    pair = tok_row // 2
    side = mdl_row // half_mdl

    swap = [
        ((a * half_tok + i) * groups + b * half_mdl + z, (b * half_tok + i) * groups + a * half_mdl + z)
        for a in range(2)
        for b in range(2)
        for i in range(half_tok)
        for z in range(half_mdl)
    ]
    out_block = lax.ppermute(out_weight, ("tok", "mdl"), swap)
    blocks = jnp.concatenate([query_weight, out_block], axis=0)
    gathered = lax.all_gather(blocks, "tok", axis=0)

    same_core = [[2 * k + c for k in range(half_tok)] for c in range(2)]
    core_swap = [(i, i ^ 1) for i in range(shards)]
    kv_mine = lax.all_to_all(
        jnp.broadcast_to(kv_weight[None], (half_tok,) + kv_weight.shape),
        "tok", 0, 0, axis_index_groups=same_core, tiled=True,
    )
    kv_other = lax.ppermute(kv_mine, "tok", core_swap)
    first = core == 0
    kv_blocks = jnp.stack(
        [jnp.where(first, kv_mine, kv_other), jnp.where(first, kv_other, kv_mine)], axis=1
    )
    kv_full = kv_blocks.transpose(0, 1, 3, 2, 4).reshape(width, 2 * head_cols)
    normed = rms_norm(hidden, norm_gain)
    key_values = jnp.dot(normed, kv_full, preferred_element_type=jnp.float32).astype(jnp.bfloat16)

    earlier = [
        lax.ppermute(key_values, "tok", [(i, i + 2 * s) for i in range(shards - 2 * s)])
        for s in range(WINDOW_PAIRS - 1, 0, -1)
    ]
    mine = jnp.stack(earlier + [key_values])
    other = lax.ppermute(mine, "tok", core_swap)
    window = jnp.stack(
        [jnp.where(first, mine, other), jnp.where(first, other, mine)], axis=1
    ).reshape(2 * WINDOW_PAIRS * tok_dev, 2 * head_cols)
    cache = place_pages(key_values, page_table, shards, tok_row)

    window_first = (pair - (WINDOW_PAIRS - 1)) * 2 * tok_dev
    own_first = tok_row * tok_dev
    own_segments = lax.dynamic_slice_in_dim(segment_ids, own_first, tok_dev)
    prompt_ids = jnp.arange(SEGS, dtype=jnp.int32)
    seg_first = jnp.sum((segment_ids[:, None] < prompt_ids[None, :]).astype(jnp.int32), axis=0)
    lower = jnp.sum(
        jnp.where(own_segments[:, None] == prompt_ids[None, :], seg_first[None, :], 0), axis=1
    )
    place = own_first + jnp.arange(tok_dev, dtype=jnp.int32)
    gates = route_weights(normed, router_weight, routes)

    queries = project_queries(normed, gathered, routes, experts)
    attended = attend(queries, lower - window_first, place - window_first, window)
    peer = lax.ppermute(attended, "mdl", [(j, j ^ half_mdl) for j in range(groups)])
    partial_sums = mix_heads(
        side[None],
        attended,
        peer,
        gates,
        gathered.reshape(2, half_tok, 2 * experts, chunk, head_cols),
        experts,
    )
    sides = [[b * half_mdl + z for z in range(half_mdl)] for b in range(2)]
    arrived = lax.all_to_all(partial_sums, "mdl", 0, 0, axis_index_groups=sides, tiled=True)
    mixed = jnp.sum(arrived.astype(jnp.float32), axis=0)
    span = width // groups
    residual = lax.dynamic_slice_in_dim(hidden, mdl_row * span, span, 1)
    output = (residual.astype(jnp.float32) + mixed).astype(jnp.bfloat16)
    return (output, cache)


def solution(mesh):
    placed = (
        P("tok", None),
        P(),
        P("tok", None),
        P(),
        P(),
        P(None, "tok", "mdl"),
        P(None, "tok", "mdl"),
        P(None, "mdl", "tok"),
        P("tok"),
    )
    return jax.shard_map(
        local,
        mesh=mesh,
        in_specs=placed,
        out_specs=(P("tok", "mdl"), P("tok", None, None, "mdl")),
        check_vma=False,
    )
```

time: 477 us -> 185 us (0.39); the launches traced: 470 us -> 184 us
  waiting for transfers between devices: 251 us -> 68.6 us
  other arithmetic: 69.7 us -> 12.7 us
  matrix products: 56.2 us -> 3.17 us
  local copies, waits for them, and re-layouts: 67.9 us -> 17 us
  starting transfers between devices: 10 us -> 39.8 us
  Pallas kernels: 0 us -> 27.9 us
    unnamed x6 -> x1, waiting for transfers between devices: 174 us -> 0.02 us
    all_gather x4 -> x1, waiting for transfers between devices: 67.3 us -> 5.38 us  [local(): gathered = lax.all_gather(blocks, 'tok', axis=0)]
    dot_general x36 -> x2, matrix products: 56.2 us -> 3.17 us  [the longest x1 1.72 us: route_weights(): jnp.dot(normed.astype(jnp.float32), router_weight, precision=lax.Precisio...]
    ppermute x0 -> x8, waiting for transfers between devices: none -> 31.7 us  [the longest x4 22.5 us: local(): lax.ppermute(key_values, 'tok', [(i, i + 2 * s) for i in range(shards - 2...]
    all_to_all x0 -> x2, waiting for transfers between devices: none -> 31.5 us  [the longest x1 26.4 us: local(): lax.all_to_all(partial_sums, 'mdl', 0, 0, axis_index_groups=sides, tiled=...]
    scatter-add x1 -> x0, other arithmetic: 29.5 us -> none  [local(): jnp.zeros((tok_dev, count), jnp.float32).at[slot_token]]
    pallas_call x0 -> x3, Pallas kernels: none -> 27.9 us  [the longest x1 13.7 us: attend(): pl.pallas_call(attend_body, grid_spec=pltpu.PrefetchScalarGridSpec(num_sc...]
    gather x5 -> x2, local copies, waits for them, and re-layouts: 27.9 us -> 2.81 us  [the longest x1 2.21 us: place_pages(): key_values.reshape(pages_here, rows, cols)[ordering]]
  transfers between devices with their start and end apart: 7 -> 13, of which waited for: 5 -> 6; matrix products, arithmetic and copies ran while one was open for 31% -> 15% of each run, Pallas kernels for 0% -> 15%
where the time goes in v1:
time: 185 us; the launch traced here: 184 us
  waiting for transfers between devices  68.6 us (37%)
  starting transfers between devices  39.8 us (22%)
  Pallas kernels  27.9 us (15%)
  local copies, waits for them, and re-layouts  17 us (9%)
  between operations  14.4 us (8%)
  other arithmetic  12.7 us (7%)
  matrix products  3.17 us (2%)
    all_to_all x1, waiting for transfers between devices, local(): lax.all_to_all(partial_sums, 'mdl', 0, 0, axis_index_groups=sides, tiled=...  26.4 us
    ppermute x4, waiting for transfers between devices, local(): lax.ppermute(key_values, 'tok', [(i, i + 2 * s) for i in range(shards - 2...  22.5 us
    pallas_call x1, Pallas kernels, attend(): pl.pallas_call(attend_body, grid_spec=pltpu.PrefetchScalarGridSpec(num_sc...  13.7 us
    ppermute x4, starting transfers between devices, local(): lax.ppermute(key_values, 'tok', [(i, i + 2 * s) for i in range(shards - 2...  9.53 us
    all_to_all x1, starting transfers between devices, local(): lax.all_to_all(partial_sums, 'mdl', 0, 0, axis_index_groups=sides, tiled=...  8.59 us
    pallas_call x1, Pallas kernels, mix_heads(): pl.pallas_call(mix_body, grid_spec=pltpu.PrefetchScalarGridSpec(num_scala...  8.02 us
    pallas_call x1, Pallas kernels, project_queries(): pl.pallas_call(query_body, grid=(experts // 2,), in_specs=[pl.BlockSpec((...  6.18 us
    ppermute x1, waiting for transfers between devices, local(): out_block = lax.ppermute(out_weight, ('tok', 'mdl'), swap)  6.07 us
  transfers between devices with their start and end apart: 13, of which 6 were waited for; matrix products, arithmetic and copies ran while one was open for 15% of the time, Pallas kernels for 15%

profile of v1, /device:TPU:9, one launch (start us, length us, event | category | flops | bytes accessed | tf_op | source)
XLA Modules:
  0.0 183.6 jit_solution(3152959565831181391)
XLA Ops:
  7.3 3.3 %collective-permute-start = (bf16[8,128,128]{2,1,0:T(8,128)(2,1)}, bf16[8,128,128]{2,1,0:T(8,128)(2,1)S(1)}, u32[]{:S(2)}, u32[]{:S(2)}) collective-permute-start(bf16[8,128,128]{2,1,0:T(8,128)(2,1)} %param.16), channel_id=1, source_target_pairs={{0,0},{1,1},{2,2},{3,3},{4,4},{5,5},{6,6},{7,7},{16,16},{17,17},{1... | collective-permute-start | bytes 786440 | tf_op jit(solution)/shard_map/ppermute | solution.py:242
  10.6 6.1 %collective-permute-done = bf16[8,128,128]{2,1,0:T(8,128)(2,1)S(1)} collective-permute-done((bf16[8,128,128]{2,1,0:T(8,128)(2,1)}, bf16[8,128,128]{2,1,0:T(8,128)(2,1)S(1)}, u32[]{:S(2)}, u32[]{:S(2)}) %collective-permute-start) | collective-permute-done | bytes 262176 | tf_op jit(solution)/shard_map/ppermute | solution.py:242
  16.7 1.8 %pad_maximum_fusion.2 = bf16[16,128,128]{2,1,0:T(8,128)(2,1)} fusion(bf16[8,128,128]{2,1,0:T(8,128)(2,1)S(1)} %collective-permute-done, bf16[8,128,128]{2,1,0:T(8,128)(2,1)} %param.14), kind=kLoop, calls=%fused_computation.22 | loop fusion | flops 262144 | bytes 1048576 | tf_op jit(solution)/shard_map/concatenate | solution.py:243
  20.6 5.2 %all-to-all-start = ((bf16[8,2,128,128]{3,1,2,0:T(2,128)(2,1)}), bf16[8,2,128,128]{3,1,2,0:T(2,128)(2,1)S(1)}, u32[]{:S(2)}, u32[]{:S(2)}) async-start(bf16[8,2,128,128]{3,1,2,0:T(2,128)(2,1)} %broadcast_in_dim.78), calls=%async_computation | async-start | bytes 1048576 | tf_op jit(solution)/shard_map/all_to_all | solution.py:248
  29.1 5.1 %all-to-all-done = bf16[8,2,128,128]{3,1,2,0:T(2,128)(2,1)S(1)} async-done(((bf16[8,2,128,128]{3,1,2,0:T(2,128)(2,1)}), bf16[8,2,128,128]{3,1,2,0:T(2,128)(2,1)S(1)}, u32[]{:S(2)}, u32[]{:S(2)}) %all-to-all-start) | async-done | bytes 524320 | tf_op jit(solution)/shard_map/all_to_all | solution.py:248
  34.2 5.9 %all-to-all-start.3 = ((s32[16,1,2]{2,1,0:T(1,128)}), s32[16,1,2]{2,1,0:T(1,128)S(1)}, u32[]{:S(2)}, u32[]{:S(2)}) async-start(s32[16,1,2]{2,1,0:T(1,128)} %bitcast.20), calls=%async_computation.3 | async-start | bytes 16384 | tf_op jit(solution)/shard_map/all_to_all | solution.py:53
  40.4 2.2 %fusion.2.normed_ref = bf16[512,2048]{1,0:T(8,128)(2,1)S(1)} fusion(bf16[512,2048]{1,0:T(8,128)(2,1)} %param.9, f32[2048]{0:T(1024)S(1)} %copy-done.7, f32[512]{0:T(512)S(1)} %add_rsqrt_fusion), kind=kLoop, calls=%fused_computation.9 | loop fusion | flops 4194304 | bytes 4204544 | tf_op jit(solution)/shard_map/convert_element_type | solution.py:23
  47.8 4.3 %collective-permute-start.3 = (bf16[512,256]{1,0:T(8,128)(2,1)}, bf16[512,256]{1,0:T(8,128)(2,1)}, u32[]{:S(2)}, u32[]{:S(2)}) collective-permute-start(bf16[512,256]{1,0:T(8,128)(2,1)} %convolution_convert_fusion), channel_id=1, source_target_pairs={{0,96},{16,112},{32,128},{48,144},{64,160},{80,176},{96,192},{112,... | collective-permute-start | bytes 786440 | tf_op jit(solution)/shard_map/ppermute | solution.py:262
  53.0 1.9 %collective-permute-start.4 = (bf16[512,256]{1,0:T(8,128)(2,1)}, bf16[512,256]{1,0:T(8,128)(2,1)S(1)}, u32[]{:S(2)}, u32[]{:S(2)}) collective-permute-start(bf16[512,256]{1,0:T(8,128)(2,1)} %convolution_convert_fusion), channel_id=1, source_target_pairs={{0,64},{16,80},{32,96},{48,112},{64,128},{80,144},{96,160},{112,17... | collective-permute-start | bytes 786440 | tf_op jit(solution)/shard_map/ppermute | solution.py:262
  54.9 1.9 %collective-permute-start.5 = (bf16[512,256]{1,0:T(8,128)(2,1)}, bf16[512,256]{1,0:T(8,128)(2,1)S(1)}, u32[]{:S(2)}, u32[]{:S(2)}) collective-permute-start(bf16[512,256]{1,0:T(8,128)(2,1)} %convolution_convert_fusion), channel_id=1, source_target_pairs={{0,32},{16,48},{32,64},{48,80},{64,96},{80,112},{96,128},{112,144}... | collective-permute-start | bytes 786440 | tf_op jit(solution)/shard_map/ppermute | solution.py:262
  56.8 22.5 %collective-permute-done.2 = bf16[512,256]{1,0:T(8,128)(2,1)} collective-permute-done((bf16[512,256]{1,0:T(8,128)(2,1)}, bf16[512,256]{1,0:T(8,128)(2,1)}, u32[]{:S(2)}, u32[]{:S(2)}) %collective-permute-start.2) | collective-permute-done | bytes 262176 | tf_op jit(solution)/shard_map/ppermute | solution.py:262
  85.2 1.7 fusion.17
  87.8 2.2 %gather_fusion = bf16[32,16,256]{2,1,0:T(8,128)(2,1)} fusion(bf16[32,16,256]{2,1,0:T(8,128)(2,1)} %bitcast.18, s32[1024]{0:T(1024)S(1)} %pad_clamp_fusion.1), kind=kCustom, calls=%fused_computation | custom fusion | bytes 524416 | tf_op jit(solution)/shard_map/gather | solution.py:48
  91.7 1.8 copy.45
  93.5 5.4 %all-gather.3.cloned.1.call-done = bf16[256,128,128]{2,1,0:T(8,128)(2,1)} async-done(((bf16[16,128,128]{2,1,0:T(8,128)(2,1)}), bf16[256,128,128]{2,1,0:T(8,128)(2,1)}) %all-gather.3.cloned.1.call-update) | async-done | bytes 8388624 | tf_op jit(solution)/shard_map/all_gather | solution.py:244
  98.9 6.2 %shard_map.104.q_ref = bf16[2,512,128]{2,1,0:T(8,128)(2,1)} custom-call(bf16[512,2048]{1,0:T(8,128)(2,1)} %copy-done.2, bf16[16,16,128,128]{3,2,1,0:T(8,128)(2,1)} %bitcast.45, s32[512,2]{1,0:T(8,128)} %copy.42.routes_ref), custom_call_target="tpu_custom_call" | custom-call | tf_op jit(solution)/shard_map/pallas_call | solution.py:80
  105.1 13.7 %shard_map.105.own_ref = bf16[2,512,128]{2,1,0:T(8,128)(2,1)} custom-call(s32[8]{0:T(128)} %reshape.134.bounds_ref, bf16[2,512,128]{2,1,0:T(8,128)(2,1)} %shard_map.104.q_ref, s32[512,1]{1,0:T(8,128)} %copy.46.lower_ref, s32[512,1]{1,0:T(8,128)} %add_subtract_fusion.place_ref, bf16[5120,256]{1,0:T(8,128)(2,1)} %bitcast.48), custom_call_target="tpu_custom_call" | custom-call | tf_op jit(solution)/shard_map/pallas_call | solution.py:146
  118.8 2.3 %collective-permute-start.7 = (bf16[2,512,128]{2,1,0:T(8,128)(2,1)}, bf16[2,512,128]{2,1,0:T(8,128)(2,1)S(1)}, u32[]{:S(2)}, u32[]{:S(2)}) collective-permute-start(bf16[2,512,128]{2,1,0:T(8,128)(2,1)} %shard_map.105.own_ref), channel_id=1, source_target_pairs={{0,8},{1,9},{2,10},{3,11},{4,12},{5,13},{6,14},{7,15},{8,0},{9,1},... | collective-permute-start | bytes 786440 | tf_op jit(solution)/shard_map/ppermute | solution.py:285
  121.1 3.5 %all-to-all-start.2 = ((bf16[16,2,16,256]{3,2,1,0:T(8,128)(2,1)}), bf16[16,2,16,256]{3,2,1,0:T(8,128)(2,1)S(1)}, u32[]{:S(2)}, u32[]{:S(2)}) async-start(bf16[16,2,16,256]{3,2,1,0:T(8,128)(2,1)} %bitcast.19), calls=%async_computation.2 | async-start | bytes 524288 | tf_op jit(solution)/shard_map/all_to_all | solution.py:52
  125.7 3.1 %collective-permute-done.7.peer_ref = bf16[2,512,128]{2,1,0:T(8,128)(2,1)S(1)} collective-permute-done((bf16[2,512,128]{2,1,0:T(8,128)(2,1)}, bf16[2,512,128]{2,1,0:T(8,128)(2,1)S(1)}, u32[]{:S(2)}, u32[]{:S(2)}) %collective-permute-start.7) | collective-permute-done | bytes 262176 | tf_op jit(solution)/shard_map/ppermute | solution.py:285
  129.5 8.0 %shard_map.106 = bf16[8,512,128]{2,1,0:T(8,128)(2,1)} custom-call(s32[1]{0:T(128)} %bitcast.side_ref, bf16[2,512,128]{2,1,0:T(8,128)(2,1)} %shard_map.105.own_ref, bf16[2,512,128]{2,1,0:T(8,128)(2,1)} %copy-done.4, f32[512,16]{1,0:T(8,128)} %compare_select_fusion.gates_ref, bf16[2,8,16,128,128]{4,3,2,1,0:T(8,128)(2,1)} %bitcast.46, ...), custom_call_target="tpu_custom_call" | custom-call | tf_op jit(solution)/shard_map/pallas_call | solution.py:194
  137.5 8.6 %all-to-all-start.1 = ((bf16[8,512,128]{2,1,0:T(8,128)(2,1)}), bf16[8,512,128]{2,1,0:T(8,128)(2,1)S(1)}, u32[]{:S(2)}, u32[]{:S(2)}) async-start(bf16[8,512,128]{2,1,0:T(8,128)(2,1)} %shard_map.106), calls=%async_computation.1 | async-start | bytes 2097152 | tf_op jit(solution)/shard_map/all_to_all | solution.py:295
  148.6 26.4 %all-to-all-done.1 = bf16[8,512,128]{2,1,0:T(8,128)(2,1)S(1)} async-done(((bf16[8,512,128]{2,1,0:T(8,128)(2,1)}), bf16[8,512,128]{2,1,0:T(8,128)(2,1)S(1)}, u32[]{:S(2)}, u32[]{:S(2)}) %all-to-all-start.1) | async-done | bytes 1048608 | tf_op jit(solution)/shard_map/all_to_all | solution.py:295
  175.2 1.6 add_convert_fusion
  (88 shorter events, 24.5 us)
Async XLA Ops:
  7.2 78.0 %copy-start = (f32[2048,8]{0,1:T(8,128)S(1)}, f32[2048,8]{0,1:T(8,128)}, u32[]{:S(2)}) copy-start(f32[2048,8]{0,1:T(8,128)} %param.13) | copy-start | bytes 196612
  7.2 18.6 %copy-start.1 = (s32[32]{0:T(128)S(1)}, s32[32]{0:T(128)}, u32[]{:S(2)}) copy-start(s32[32]{0:T(128)} %param.17) | copy-start | bytes 388
  7.2 21.0 %copy-start.5 = (s32[8192]{0:T(1024)S(1)}, s32[8192]{0:T(1024)}, u32[]{:S(2)}) copy-start(s32[8192]{0:T(1024)} %param.10) | copy-start | bytes 98308
  7.2 21.4 %copy-start.3 = (bf16[512,2048]{1,0:T(8,128)(2,1)S(1)}, bf16[512,2048]{1,0:T(8,128)(2,1)}, u32[]{:S(2)}) copy-start(bf16[512,2048]{1,0:T(8,128)(2,1)} %param.9) | copy-start | bytes 6291460
  7.2 91.7 %all-gather.3.cloned.1.call-start = ((), (), s32[]{:S(2)}) async-start(), calls=%async_computation.4 | async-start | bytes 8912896 | tf_op jit(solution)/shard_map/all_gather | solution.py:244
  7.3 9.4 %collective-permute-start = (bf16[8,128,128]{2,1,0:T(8,128)(2,1)}, bf16[8,128,128]{2,1,0:T(8,128)(2,1)S(1)}, u32[]{:S(2)}, u32[]{:S(2)}) collective-permute-start(bf16[8,128,128]{2,1,0:T(8,128)(2,1)} %param.16), channel_id=1, source_target_pairs={{0,0},{1,1},{2,2},{3,3},{4,4},{5,5},{6,6},{7,7},{16,16},{17,17},{1... | collective-permute-start | bytes 786440 | tf_op jit(solution)/shard_map/ppermute | solution.py:242
  19.4 21.0 %copy-start.7 = (f32[2048]{0:T(1024)S(1)}, f32[2048]{0:T(1024)}, u32[]{:S(2)}) copy-start(f32[2048]{0:T(1024)} %param.12) | copy-start | bytes 24580
  20.6 13.6 %all-to-all-start = ((bf16[8,2,128,128]{3,1,2,0:T(2,128)(2,1)}), bf16[8,2,128,128]{3,1,2,0:T(2,128)(2,1)S(1)}, u32[]{:S(2)}, u32[]{:S(2)}) async-start(bf16[8,2,128,128]{3,1,2,0:T(2,128)(2,1)} %broadcast_in_dim.78), calls=%async_computation | async-start | bytes 1048576 | tf_op jit(solution)/shard_map/all_to_all | solution.py:248
  34.2 86.9 %all-to-all-start.3 = ((s32[16,1,2]{2,1,0:T(1,128)}), s32[16,1,2]{2,1,0:T(1,128)S(1)}, u32[]{:S(2)}, u32[]{:S(2)}) async-start(s32[16,1,2]{2,1,0:T(1,128)} %bitcast.20), calls=%async_computation.3 | async-start | bytes 16384 | tf_op jit(solution)/shard_map/all_to_all | solution.py:53
  40.0 2.6 %collective-permute-start.1 = (bf16[8,2,128,128]{3,1,2,0:T(2,128)(2,1)S(1)}, bf16[8,2,128,128]{3,1,2,0:T(2,128)(2,1)S(1)}, u32[]{:S(2)}, u32[]{:S(2)}) collective-permute-start(bf16[8,2,128,128]{3,1,2,0:T(2,128)(2,1)S(1)} %all-to-all-done), channel_id=1, source_target_pairs={{0,16},{16,0},{32,48},{48,32},{64,80},{80,64},{96,112},{112,96},{1... | collective-permute-start | bytes 1572872 | tf_op jit(solution)/shard_map/ppermute | solution.py:252
  42.6 42.6 %copy-start.2 = (bf16[512,2048]{1,0:T(8,128)(2,1)}, bf16[512,2048]{1,0:T(8,128)(2,1)S(1)}, u32[]{:S(2)}) copy-start(bf16[512,2048]{1,0:T(8,128)(2,1)S(1)} %fusion.2.normed_ref) | copy-start | bytes 6291460
  46.4 38.0 %copy-start.6 = (s32[512,2]{0,1:T(2,128)S(1)}, s32[512,2]{0,1:T(2,128)}, u32[]{:S(2)}) copy-start(s32[512,2]{0,1:T(2,128)} %param.11) | copy-start | bytes 12292
  46.4 32.9 %collective-permute-start.2 = (bf16[512,256]{1,0:T(8,128)(2,1)}, bf16[512,256]{1,0:T(8,128)(2,1)}, u32[]{:S(2)}, u32[]{:S(2)}) collective-permute-start(bf16[512,256]{1,0:T(8,128)(2,1)} %convolution_convert_fusion), channel_id=1, source_target_pairs={{0,128},{16,144},{32,160},{48,176},{64,192},{80,208},{96,224},{112... | collective-permute-start | bytes 786440 | tf_op jit(solution)/shard_map/ppermute | solution.py:262
  47.8 32.5 %collective-permute-start.3 = (bf16[512,256]{1,0:T(8,128)(2,1)}, bf16[512,256]{1,0:T(8,128)(2,1)}, u32[]{:S(2)}, u32[]{:S(2)}) collective-permute-start(bf16[512,256]{1,0:T(8,128)(2,1)} %convolution_convert_fusion), channel_id=1, source_target_pairs={{0,96},{16,112},{32,128},{48,144},{64,160},{80,176},{96,192},{112,... | collective-permute-start | bytes 786440 | tf_op jit(solution)/shard_map/ppermute | solution.py:262
  53.0 28.3 %collective-permute-start.4 = (bf16[512,256]{1,0:T(8,128)(2,1)}, bf16[512,256]{1,0:T(8,128)(2,1)S(1)}, u32[]{:S(2)}, u32[]{:S(2)}) collective-permute-start(bf16[512,256]{1,0:T(8,128)(2,1)} %convolution_convert_fusion), channel_id=1, source_target_pairs={{0,64},{16,80},{32,96},{48,112},{64,128},{80,144},{96,160},{112,17... | collective-permute-start | bytes 786440 | tf_op jit(solution)/shard_map/ppermute | solution.py:262
  54.9 26.4 %collective-permute-start.5 = (bf16[512,256]{1,0:T(8,128)(2,1)}, bf16[512,256]{1,0:T(8,128)(2,1)S(1)}, u32[]{:S(2)}, u32[]{:S(2)}) collective-permute-start(bf16[512,256]{1,0:T(8,128)(2,1)} %convolution_convert_fusion), channel_id=1, source_target_pairs={{0,32},{16,48},{32,64},{48,80},{64,96},{80,112},{96,128},{112,144}... | collective-permute-start | bytes 786440 | tf_op jit(solution)/shard_map/ppermute | solution.py:262
  82.4 7.6 %collective-permute-start.6 = (bf16[5,512,256]{2,1,0:T(8,128)(2,1)S(1)}, bf16[5,512,256]{2,1,0:T(8,128)(2,1)}, u32[]{:S(2)}, u32[]{:S(2)}) collective-permute-start(bf16[5,512,256]{2,1,0:T(8,128)(2,1)S(1)} %bitcast_dynamic-update-slice_fusion), channel_id=1, source_target_pairs={{0,16},{16,0},{32,48},{48,32},{64,80},{80,64},{96,112},{112,96},{1... | collective-permute-start | bytes 3932168 | tf_op jit(solution)/shard_map/ppermute | solution.py:266
  118.8 10.0 %collective-permute-start.7 = (bf16[2,512,128]{2,1,0:T(8,128)(2,1)}, bf16[2,512,128]{2,1,0:T(8,128)(2,1)S(1)}, u32[]{:S(2)}, u32[]{:S(2)}) collective-permute-start(bf16[2,512,128]{2,1,0:T(8,128)(2,1)} %shard_map.105.own_ref), channel_id=1, source_target_pairs={{0,8},{1,9},{2,10},{3,11},{4,12},{5,13},{6,14},{7,15},{8,0},{9,1},... | collective-permute-start | bytes 786440 | tf_op jit(solution)/shard_map/ppermute | solution.py:285
  121.1 16.5 %all-to-all-start.2 = ((bf16[16,2,16,256]{3,2,1,0:T(8,128)(2,1)}), bf16[16,2,16,256]{3,2,1,0:T(8,128)(2,1)S(1)}, u32[]{:S(2)}, u32[]{:S(2)}) async-start(bf16[16,2,16,256]{3,2,1,0:T(8,128)(2,1)} %bitcast.19), calls=%async_computation.2 | async-start | bytes 524288 | tf_op jit(solution)/shard_map/all_to_all | solution.py:52
  128.8 0.7 copy-start.4
  137.5 37.5 %all-to-all-start.1 = ((bf16[8,512,128]{2,1,0:T(8,128)(2,1)}), bf16[8,512,128]{2,1,0:T(8,128)(2,1)S(1)}, u32[]{:S(2)}, u32[]{:S(2)}) async-start(bf16[8,512,128]{2,1,0:T(8,128)(2,1)} %shard_map.106), calls=%async_computation.1 | async-start | bytes 2097152 | tf_op jit(solution)/shard_map/all_to_all | solution.py:295
Sparse Core Ops, SparseCore 0:
  18.7 80.1 all-gather.2
